TPU v7x, 256 devices: a whole 4x4x8 slice. The times are simulated.
256 devices in a mesh: dp: 2 (over core), ctx: 16 (over z_hi, y), exp: 8 (over x, z_lo).
Axes of the slice: x: 4, y: 4, z: 8 (z_hi: 4, z_lo: 2; z = z_hi * 2 + z_lo), core: 2. Of those that a mesh axis runs over, the one named last changes fastest.
Arguments:
- tokens: bfloat16 [2, 2048, 2560], P('dp', 'ctx'), may hold values from -6 to 6
- queries: bfloat16 [2, 2048, 16, 576], P('dp', 'ctx', 'exp'), may hold values from -240 to 240
- kv_weight: bfloat16 [2560, 576], P('exp'), may hold values from -0.125 to 0.125
- kv_gain: bfloat16 [512], replicated, may hold values from 0.5 to 1.5
- uv_weight: bfloat16 [16, 512, 128], P('exp'), may hold values from -0.75 to 0.75
- out_weight: bfloat16 [2048, 2560], P('exp'), may hold values from -0.5 to 0.5
- post_gain: bfloat16 [2560], replicated, may hold values from 0.5 to 1.5
- router_weight: bfloat16 [2560, 32], replicated, may hold values from -0.125 to 0.125
- expert_ids: int32 [2, 2048, 6], P('dp', 'ctx'), may hold values from 0 to 31, all different within a row; in each aligned block of 128 rows (0 to 127, 128 to 255, ..., all dimensions but the last counted through in order) at most 32 rows name the same one
- doc_ids: int32 [2, 2048], P('dp', 'ctx'), may hold values from 0 to 3, never falling along the last dimension, each value on 1 to 1024 neighbouring positions
- gate_weight: bfloat16 [32, 2560, 1536], P('ctx', None, 'exp'), may hold values from -0.125 to 0.125
- up_weight: bfloat16 [32, 2560, 1536], P('ctx', None, 'exp'), may hold values from -0.125 to 0.125
- down_weight: bfloat16 [32, 1536, 2560], P('ctx', 'exp'), may hold values from -0.15625 to 0.15625
- cotangent: bfloat16 [2, 2048, 2560], P('dp', 'ctx'), may hold values from -6 to 6
Outputs:
- layer_out: bfloat16 [2, 2048, 2560], P('dp', 'ctx')
- router_grad: float32 [2560, 32], replicated
- gate_grad: bfloat16 [32, 2560, 1536], P('ctx', 'dp', 'exp')
- up_grad: bfloat16 [32, 2560, 1536], P('ctx', 'dp', 'exp')
- down_grad: bfloat16 [32, 1536, 2560], P('ctx', 'exp', 'dp')
Inputs may be any that keep to these rules, and one draw needn't show every extreme that they name: `expert_ids`: in each aligned block of 128 positions of a sequence no expert is named by more than 32 of the block's assignments; the experts of one token differ. `doc_ids`: document numbers never fall along a sequence; a document has at most 1024 positions.
All inputs are finite; a program needn't handle non-finite values.
Results may differ from a plain program's by a relative error of at most 0.023.
The roundings to bfloat16 on the way count: a program that leaves them out, or rounds other values in their place, can miss the bound.
Values may be sent and summed in bfloat16 or wider, within the bound.
No kernel may reach another device: no remote copies, remote signals or barrier semaphores. Data moves between devices by JAX's collectives and lax.ppermute only.
A program may use at most 128 MiB of HBM per device.

v0:
```python
import jax
import jax.numpy as jnp
from jax import lax
from jax.sharding import PartitionSpec as P

ROPE = 64
NOPE = 128
epsilon = 1e-06


def from_everyone(array, axis):
    count = lax.axis_size(axis)
    return lax.all_to_all(
        jnp.broadcast_to(array[None], (count, *array.shape)), axis, 0, 0, tiled=True
    )


def taken_together(array, axis):
    everything = from_everyone(array, axis)
    return jnp.sum(everything, axis=0)


def in_one_piece(arrays, axis, split_dim, concat_dim, along):
    both = jnp.concatenate(arrays, axis=along)
    result, at, gathered = (
        lax.all_to_all(both, axis, split_axis=split_dim, concat_axis=concat_dim, tiled=True),
        0,
        [],
    )
    for a in arrays:
        gathered.append(lax.slice_in_dim(result, at, at + a.shape[along], axis=along))
        at += a.shape[along]
    return tuple(gathered)


def rms_scale(values, gain):
    return values * lax.rsqrt(jnp.mean(values * values, axis=-1, keepdims=True) + epsilon) * gain


def rotate(rope_part, positions):
    half_width = rope_part.shape[-1] // 2
    frequency = jnp.power(
        10000.0, -2.0 * jnp.arange(half_width, dtype=jnp.float32) / rope_part.shape[-1]
    )
    angles = positions.astype(jnp.float32)[:, None] * frequency[None, :]
    cosine = jnp.cos(angles)
    sine_part = jnp.sin(angles)
    first_half = rope_part[:, :half_width]
    second = rope_part[:, half_width:]
    return jnp.concatenate(
        [first_half * cosine - second * sine_part, second * cosine + first_half * sine_part], axis=1
    )


def route_slots(outgoing):
    moved = lax.all_to_all(outgoing, ("dp", "ctx"), split_axis=0, concat_axis=0, tiled=True)
    return moved


def local(
    tokens,
    queries,
    kv_weight,
    kv_gain,
    uv_weight,
    out_weight,
    post_gain,
    router_weight,
    expert_ids,
    doc_ids,
    gate_weight,
    up_weight,
    down_weight,
    cotangent,
):
    local_rows = tokens[0]
    seq_rows = local_rows.shape[0]
    model_width = local_rows.shape[1]
    latent_width = kv_gain.shape[0]
    row_share = kv_weight.shape[0]
    columns = lax.dynamic_slice_in_dim(local_rows, lax.axis_index("exp") * row_share, row_share, 1)
    compressed = taken_together(
        jnp.dot(columns, kv_weight, preferred_element_type=jnp.float32), "exp"
    )
    positions = lax.axis_index("ctx") * seq_rows + jnp.arange(seq_rows, dtype=jnp.int32)
    latent = rms_scale(compressed[:, :latent_width], kv_gain.astype(jnp.float32)).astype(
        jnp.bfloat16
    )
    rope_key = rotate(compressed[:, latent_width:], positions).astype(jnp.bfloat16)
    key_rows = jnp.concatenate([latent, rope_key], axis=1)
    all_keys, all_docs = (
        lax.all_gather(key_rows, "ctx", axis=0, tiled=True),
        lax.all_gather(doc_ids[0], "ctx", axis=0, tiled=True),
    )
    key_positions = jnp.arange(all_keys.shape[0], dtype=jnp.int32)
    allowed = (key_positions[None, :] <= positions[:, None]) & (
        all_docs[None, :] == doc_ids[0][:, None]
    )
    allowed = allowed[:, None, :]
    score_scale = (NOPE + ROPE) ** (-0.5)
    scores = (
        jnp.einsum("qhd,kd->qhk", queries[0], all_keys, preferred_element_type=jnp.float32)
        * score_scale
    )
    score_peak = jnp.max(jnp.where(allowed, scores, -1e30), axis=-1, keepdims=True)
    weights = jnp.exp(jnp.where(allowed, scores - score_peak, -1e30))
    weight_total = jnp.sum(weights, axis=-1, keepdims=True)
    mixed_latent = (
        jnp.einsum(
            "qhk,kl->qhl",
            weights.astype(jnp.bfloat16),
            all_keys[:, :latent_width],
            preferred_element_type=jnp.float32,
        )
        / weight_total
    )
    mixed_latent = mixed_latent.astype(jnp.bfloat16)
    head_values = (
        jnp.einsum("qhl,hlv->qhv", mixed_latent, uv_weight, preferred_element_type=jnp.float32)
        .astype(jnp.bfloat16)
        .reshape(seq_rows, -1)
    )
    head_part = jnp.dot(head_values, out_weight, preferred_element_type=jnp.float32)
    attention = lax.psum(head_part, "exp")
    hidden = (local_rows.astype(jnp.float32) + attention).astype(jnp.bfloat16)
    normed = rms_scale(hidden.astype(jnp.float32), post_gain.astype(jnp.float32)).astype(
        jnp.bfloat16
    )
    logits = jnp.dot(normed, router_weight, preferred_element_type=jnp.float32)
    router_probs = jax.nn.softmax(logits, axis=-1)
    picked_ids = expert_ids[0]
    experts_all = router_weight.shape[1]
    top_count = picked_ids.shape[1]
    chosen = jnp.take_along_axis(router_probs, picked_ids, axis=1)
    chosen_sum = jnp.sum(chosen, axis=1, keepdims=True)
    route_w = chosen / chosen_sum
    route_wb = route_w.astype(jnp.bfloat16)
    ctx_count = lax.axis_size("ctx")
    held_experts = experts_all // ctx_count
    capacity = (4 * seq_rows * top_count + 3 * experts_all - 1) // (3 * experts_all)
    flat_ids = picked_ids.reshape(-1)
    onehot = (flat_ids[:, None] == jnp.arange(experts_all, dtype=jnp.int32)[None, :]).astype(
        jnp.int32
    )
    slot_rank = jnp.sum((jnp.cumsum(onehot, axis=0) - onehot) * onehot, axis=1).reshape(
        seq_rows, top_count
    )
    dp_count = lax.axis_size("dp")
    local_count = held_experts // dp_count
    first_local = lax.axis_index("dp") * local_count
    gate_local = lax.dynamic_slice_in_dim(gate_weight, first_local, local_count, 0)
    up_local = lax.dynamic_slice_in_dim(up_weight, first_local, local_count, 0)
    down_local = lax.dynamic_slice_in_dim(down_weight, first_local, local_count, 0)
    home_ctx = picked_ids // held_experts
    remainder = picked_ids % held_experts
    home_dp = remainder // local_count
    within = remainder % local_count
    slot_index = ((home_dp * ctx_count + home_ctx) * local_count + within) * capacity + slot_rank
    slot_hits = (
        slot_index[:, :, None] == jnp.arange(experts_all * capacity, dtype=jnp.int32)[None, None, :]
    )
    dispatch = jnp.any(slot_hits, axis=1).astype(jnp.bfloat16)
    combine = jnp.sum(
        jnp.where(slot_hits, route_wb[:, :, None], jnp.zeros((), jnp.bfloat16)), axis=1
    )
    outgoing = jnp.einsum("se,sd->ed", dispatch, normed, preferred_element_type=jnp.float32).astype(
        jnp.bfloat16
    )
    outgoing = outgoing.reshape(-1, local_count, capacity, model_width)
    arrived = route_slots(outgoing)
    gate_pre = jnp.einsum("sjcd,jdf->sjcf", arrived, gate_local, preferred_element_type=jnp.float32)
    up_pre = jnp.einsum("sjcd,jdf->sjcf", arrived, up_local, preferred_element_type=jnp.float32)
    activated = (jax.nn.silu(gate_pre) * up_pre).astype(jnp.bfloat16)
    expert_part = jnp.einsum(
        "sjcf,jfd->sjcd", activated, down_local, preferred_element_type=jnp.float32
    ).astype(jnp.bfloat16)
    returned = lax.all_to_all(expert_part, ("dp", "ctx"), split_axis=0, concat_axis=0, tiled=True)
    returned = returned.reshape(experts_all * capacity, model_width)
    moe_part = jnp.dot(combine, returned, preferred_element_type=jnp.float32)
    cot_rows = cotangent[0]
    cross_terms = jnp.einsum("sd,ed->se", cot_rows, returned, preferred_element_type=jnp.float32)
    dweight_part = jnp.take_along_axis(cross_terms, slot_index, axis=1)
    moe, dweight = lax.psum((moe_part, dweight_part), "exp")
    layer_out = (hidden.astype(jnp.float32) + moe).astype(jnp.bfloat16)
    mean_term = jnp.sum(dweight * route_w, axis=1, keepdims=True)
    dchosen = (dweight - mean_term) / chosen_sum
    id_hits = (
        picked_ids[:, :, None] == jnp.arange(experts_all, dtype=jnp.int32)[None, None, :]
    ).astype(jnp.float32)
    dprobs = jnp.sum(id_hits * dchosen[:, :, None], axis=1)
    dlogits = router_probs * (dprobs - jnp.sum(router_probs * dprobs, axis=1, keepdims=True))
    router_term = jnp.dot(normed.astype(jnp.float32).T, dlogits, precision=lax.Precision.HIGHEST)
    router_grad = lax.psum(router_term, ("dp", "ctx"))
    slot_cot = jnp.einsum(
        "se,sd->ed", combine, cot_rows, preferred_element_type=jnp.float32
    ).astype(jnp.bfloat16)
    slot_cot = slot_cot.reshape(-1, local_count, capacity, model_width)
    cot_arrived = route_slots(slot_cot)
    down_term = jnp.einsum(
        "sjcf,sjcd->jfd", activated, cot_arrived, preferred_element_type=jnp.float32
    )
    dact = jnp.einsum("sjcd,jfd->sjcf", cot_arrived, down_local, preferred_element_type=jnp.float32)
    sigmoid_gate = jax.nn.sigmoid(gate_pre)
    dgate = (dact * up_pre * sigmoid_gate * (1.0 + gate_pre * (1.0 - sigmoid_gate))).astype(
        jnp.bfloat16
    )
    dup = (dact * gate_pre * sigmoid_gate).astype(jnp.bfloat16)
    gate_term = jnp.einsum("sjcd,sjcf->jdf", arrived, dgate, preferred_element_type=jnp.float32)
    up_term = jnp.einsum("sjcd,sjcf->jdf", arrived, dup, preferred_element_type=jnp.float32)
    gate_out, up_out = in_one_piece(
        (gate_term.astype(jnp.bfloat16), up_term.astype(jnp.bfloat16)), "dp", 1, 0, 2
    )
    down_out = lax.all_to_all(
        down_term.astype(jnp.bfloat16), "dp", split_axis=2, concat_axis=0, tiled=True
    )
    return (layer_out[None], router_grad, gate_out, up_out, down_out)


def solution(mesh):
    placed = (
        P("dp", "ctx", None),
        P("dp", "ctx", "exp", None),
        P("exp", None),
        P(),
        P("exp", None, None),
        P("exp", None),
        P(),
        P(),
        P("dp", "ctx", None),
        P("dp", "ctx"),
        P("ctx", None, "exp"),
        P("ctx", None, "exp"),
        P("ctx", "exp", None),
        P("dp", "ctx", None),
    )
    return jax.shard_map(
        local,
        mesh=mesh,
        in_specs=placed,
        out_specs=(
            P("dp", "ctx", None),
            P(),
            P("ctx", "dp", "exp"),
            P("ctx", "dp", "exp"),
            P("ctx", "exp", "dp"),
        ),
        check_vma=False,
    )
```

profile of v0, /device:TPU:88, one launch (start us, length us, event | category | flops | bytes accessed | tf_op | source)
XLA Modules:
  0.0 998.6 jit_solution(10595866600486797685)
XLA Ops:
  10.4 5.8 all-to-all-start
  16.3 29.8 %all-to-all-done = f32[8,128,576]{1,2,0:T(8,128)} async-done(((f32[8,128,576]{1,2,0:T(8,128)}), f32[8,128,576]{1,2,0:T(8,128)}, u32[]{:S(2)}, u32[]{:S(2)}) %all-to-all-start) | async-done | bytes 2359328 | tf_op jit(solution)/shard_map/all_to_all | solution.py:13
  49.0 37.8 %all-gather = s32[1,2048]{1,0:T(1,128)S(1)} all-gather(s32[1,128]{1,0:T(1,128)S(1)} %copy-done.4), channel_id=2, replica_groups=mesh['dp'=2,'ctx'=16,'exp'=8] {'ctx'}, dimensions={1}, use_global_device_ids=true | all-gather | bytes 8704 | tf_op jit(solution)/shard_map/all_gather | solution.py:93
  87.1 26.5 %all-gather.3.cloned.1.call-done = bf16[2048,576]{0,1:T(8,128)(2,1)} async-done(((bf16[128,576]{0,1:T(8,128)(2,1)}), bf16[2048,576]{0,1:T(8,128)(2,1)}) %all-gather.3.cloned.1.call-update) | async-done | bytes 2359312 | tf_op jit(solution)/shard_map/all_gather | solution.py:92
  126.0 83.0 %all-reduce.4.cloned.1.call-done = f32[128,2560]{1,0:T(8,128)} async-done(((f32[128,2560]{1,0:T(8,128)}), f32[128,2560]{1,0:T(8,128)}) %all-reduce.4.cloned.1.call-update) | async-done | bytes 1310736 | tf_op jit(solution)/shard_map/psum | solution.py:124
  214.7 8.9 all-to-all-start.1
  223.7 113.3 %all-to-all-done.1 = bf16[32,1,32,2560]{3,2,1,0:T(8,128)(2,1)} async-done(((bf16[32,1,32,2560]{3,2,1,0:T(8,128)(2,1)}), bf16[32,1,32,2560]{3,2,1,0:T(8,128)(2,1)}, u32[]{:S(2)}, u32[]{:S(2)}) %all-to-all-start.1) | async-done | bytes 5242912 | tf_op jit(solution)/shard_map/all_to_all | solution.py:56
  341.4 5.4 multiply_convert_fusion.2
  351.4 12.1 %all-to-all-start.2 = ((bf16[32,1,32,2560]{3,2,1,0:T(8,128)(2,1)}), bf16[32,1,32,2560]{3,2,1,0:T(8,128)(2,1)}, u32[]{:S(2)}, u32[]{:S(2)}) async-start(bf16[32,1,32,2560]{3,2,1,0:T(8,128)(2,1)} %fusion.13), calls=%async_computation.2 | async-start | bytes 10485760 | tf_op jit(solution)/shard_map/all_to_all | solution.py:177
  364.6 5.1 gather_fusion
  370.0 107.0 %all-to-all-done.2 = bf16[32,1,32,2560]{3,2,1,0:T(8,128)(2,1)} async-done(((bf16[32,1,32,2560]{3,2,1,0:T(8,128)(2,1)}), bf16[32,1,32,2560]{3,2,1,0:T(8,128)(2,1)}, u32[]{:S(2)}, u32[]{:S(2)}) %all-to-all-start.2) | async-done | bytes 5242912 | tf_op jit(solution)/shard_map/all_to_all | solution.py:177
  481.1 5.1 gather_fusion.1
  486.4 23.5 %psum.30 = f32[128,6]{0,1:T(8,128)S(1)} all-reduce(f32[128,6]{0,1:T(8,128)S(1)} %and_select_fusion), channel_id=1, replica_groups=mesh['dp'=2,'ctx'=16,'exp'=8] {'exp'}, use_global_device_ids=true, to_apply=%region_15.16 | all-reduce | flops 768 | bytes 6144 | tf_op jit(solution)/shard_map/psum | solution.py:183
  510.4 5.0 convolution_convert_fusion
  515.4 9.6 all-to-all-start.3
  530.9 158.4 %all-reduce.6.cloned.1.call-done = f32[128,2560]{1,0:T(8,128)} async-done(((f32[128,2560]{1,0:T(8,128)}), f32[128,2560]{1,0:T(8,128)}) %all-reduce.6.cloned.1.call-update) | async-done | bytes 1310736 | tf_op jit(solution)/shard_map/psum | solution.py:183
  704.9 8.9 copy.117
  714.4 18.2 %reduce.3 = bf16[2560,384]{1,0:T(8,128)(2,1)} reduce(bf16[2560,1,384]{2,1,0:T(2,128)(2,1)} %bitcast.237, bf16[]{:T(256)} %broadcast.489), dimensions={1}, to_apply=%bitcast.212.reduce_sub_computation | reduce | bytes 3932162
  735.3 8.4 all_to_all.50
  760.5 6.3 copy.118
  766.8 15.4 %reduce.4 = bf16[2560,192]{1,0:T(8,128)(2,1)S(1)} reduce(bf16[2560,1,192]{2,1,0:T(2,128)(2,1)} %bitcast.241, bf16[]{:T(256)} %broadcast.489), dimensions={1}, to_apply=%bitcast.214.reduce_sub_computation | reduce | bytes 1966082
  784.5 5.6 all_to_all.51
  793.0 5.1 copy.119
  801.5 188.8 %all-reduce.8.cloned.1.call-done = f32[2560,32]{0,1:T(8,128)} async-done(((f32[2560,32]{0,1:T(8,128)}), f32[2560,32]{0,1:T(8,128)}) %all-reduce.8.cloned.1.call-update) | async-done | bytes 327696 | tf_op jit(solution)/shard_map/psum | solution.py:193
  (112 shorter events, 91.3 us)
Async XLA Ops:
  7.2 340.4 %copy-start = (bf16[2,192,2560]{2,1,0:T(8,128)(2,1)S(1)}, bf16[2,192,2560]{2,1,0:T(8,128)(2,1)}, u32[]{:S(2)}) copy-start(bf16[2,192,2560]{2,1,0:T(8,128)(2,1)} %param.26) | copy-start | bytes 5898244
  10.4 5.9 copy-start.5
  10.4 35.7 %all-to-all-start = ((f32[8,128,576]{1,2,0:T(8,128)}), f32[8,128,576]{1,2,0:T(8,128)}, u32[]{:S(2)}, u32[]{:S(2)}) async-start(f32[8,128,576]{1,2,0:T(8,128)} %broadcast_in_dim.34), calls=%async_computation | async-start | bytes 4718592 | tf_op jit(solution)/shard_map/all_to_all | solution.py:13
  16.1 32.8 %copy-start.4 = (s32[1,128]{1,0:T(1,128)S(1)}, s32[1,128]{1,0:T(1,128)}, u32[]{:S(2)}) copy-start(s32[1,128]{1,0:T(1,128)} %param.23) | copy-start | bytes 1540
  16.2 97.5 %copy-start.7 = (bf16[1,128,2,576]{1,3,2,0:T(8,128)(2,1)S(1)}, bf16[1,128,2,576]{1,3,2,0:T(8,128)(2,1)}, u32[]{:S(2)}) copy-start(bf16[1,128,2,576]{1,3,2,0:T(8,128)(2,1)} %param.15) | copy-start | bytes 884740
  16.2 97.4 %all-gather.3.cloned.1.call-start = ((), (), s32[]{:S(2)}) async-start(), calls=%async_computation.6 | async-start | bytes 2506752 | tf_op jit(solution)/shard_map/all_gather | solution.py:92
  48.9 160.1 %all-reduce.4.cloned.1.call-start = ((), (), s32[]{:S(2)}) async-start(), calls=%async_computation.7 | async-start | bytes 2621440 | tf_op jit(solution)/shard_map/psum | solution.py:124
  118.3 2.9 copy-start.1
  121.2 1.5 copy-start.2
  121.2 4.3 copy-start.3
  214.7 122.2 %all-to-all-start.1 = ((bf16[32,1,32,2560]{3,2,1,0:T(8,128)(2,1)}), bf16[32,1,32,2560]{3,2,1,0:T(8,128)(2,1)}, u32[]{:S(2)}, u32[]{:S(2)}) async-start(bf16[32,1,32,2560]{3,2,1,0:T(8,128)(2,1)} %bitcast.235), calls=%async_computation.1 | async-start | bytes 10485760 | tf_op jit(solution)/shard_map/all_to_all | solution.py:56
  336.9 4.5 copy-start.6
  341.4 5.4 copy-start.9
  346.8 0.8 copy-start.12
  351.4 12.7 %copy-start.8 = (bf16[2560,32]{0,1:T(8,128)(2,1)S(1)}, bf16[2560,32]{0,1:T(8,128)(2,1)}, u32[]{:S(2)}) copy-start(bf16[2560,32]{0,1:T(8,128)(2,1)} %param.21) | copy-start | bytes 491524
  351.4 125.5 %all-to-all-start.2 = ((bf16[32,1,32,2560]{3,2,1,0:T(8,128)(2,1)}), bf16[32,1,32,2560]{3,2,1,0:T(8,128)(2,1)}, u32[]{:S(2)}, u32[]{:S(2)}) async-start(bf16[32,1,32,2560]{3,2,1,0:T(8,128)(2,1)} %fusion.13), calls=%async_computation.2 | async-start | bytes 10485760 | tf_op jit(solution)/shard_map/all_to_all | solution.py:177
  515.4 176.2 %all-to-all-start.3 = ((bf16[32,1,32,2560]{3,2,1,0:T(8,128)(2,1)}), bf16[32,1,32,2560]{3,2,1,0:T(8,128)(2,1)}, u32[]{:S(2)}, u32[]{:S(2)}) async-start(bf16[32,1,32,2560]{3,2,1,0:T(8,128)(2,1)} %bitcast.236), calls=%async_computation.3 | async-start | bytes 10485760 | tf_op jit(solution)/shard_map/all_to_all | solution.py:56
  525.0 164.4 %all-reduce.6.cloned.1.call-start = ((), (), s32[]{:S(2)}) async-start(), calls=%async_computation.8 | async-start | bytes 2621440 | tf_op jit(solution)/shard_map/psum | solution.py:183
  529.4 460.9 %all-reduce.8.cloned.1.call-start = ((), (), s32[]{:S(2)}) async-start(), calls=%async_computation.9 | async-start | bytes 655360 | tf_op jit(solution)/shard_map/psum | solution.py:193
  691.6 4.1 copy-start.10
  695.8 3.9 copy-start.11
  748.0 2.5 copy-start.13
Sparse Core Ops, SparseCore 0:
  49.1 64.4 all-gather.2
  122.8 86.1 all-reduce.3
  529.6 159.7 all-reduce.5
  692.4 297.9 all-reduce.7
where the time goes:
time: 1000 us; the launch traced here: 999 us
  waiting for transfers between devices  707 us (71%)
  blocking collectives  75.3 us (8%)
  local copies, waits for them, and re-layouts  60.3 us (6%)
  matrix products  58.1 us (6%)
  other arithmetic  47.3 us (5%)
  starting transfers between devices  36.6 us (4%)
  between operations  14.2 us (1%)
    psum x1, waiting for transfers between devices, local(): router_grad = lax.psum(router_term, ('dp', 'ctx'))  189 us
    psum x1, waiting for transfers between devices, local(): moe, dweight = lax.psum((moe_part, dweight_part), 'exp')  158 us
    all_to_all x2, waiting for transfers between devices, route_slots(): lax.all_to_all(outgoing, ('dp', 'ctx'), split_axis=0, concat_axis=0, tile...  113 us
    all_to_all x1, waiting for transfers between devices, local(): lax.all_to_all(expert_part, ('dp', 'ctx'), split_axis=0, concat_axis=0, t...  107 us
    psum x1, waiting for transfers between devices, local(): attention = lax.psum(head_part, 'exp')  83 us
    all_gather x1, blocking collectives, local(): lax.all_gather(doc_ids[0], 'ctx', axis=0, tiled=True)  37.8 us
    unnamed x2, other arithmetic  33.5 us
    all_to_all x1, waiting for transfers between devices, from_everyone(): lax.all_to_all(jnp.broadcast_to(array[None], (count, *array.shape)), axis...  29.8 us
  transfers between devices with their start and end apart: 8, of which 7 were waited for; matrix products, arithmetic and copies ran while one was open for 11% of the time, Pallas kernels for 0%

commit v1 on v0

--- a/solution.py
+++ b/solution.py
@@ -190,7 +190,7 @@
     dprobs = jnp.sum(id_hits * dchosen[:, :, None], axis=1)
     dlogits = router_probs * (dprobs - jnp.sum(router_probs * dprobs, axis=1, keepdims=True))
     router_term = jnp.dot(normed.astype(jnp.float32).T, dlogits, precision=lax.Precision.HIGHEST)
-    router_grad = lax.psum(router_term, ("dp", "ctx"))
+    router_grad = lax.psum(lax.psum(router_term, "ctx"), "dp")
     slot_cot = jnp.einsum(
         "se,sd->ed", combine, cot_rows, preferred_element_type=jnp.float32
     ).astype(jnp.bfloat16)

time: 1000 us -> 947 us (0.947)
  waiting for transfers between devices: 707 us -> 651 us
    psum x1, waiting for transfers between devices: 158 us -> 89 us  [local(): moe, dweight = lax.psum((moe_part, dweight_part), 'exp')]
    psum x1 -> x2, waiting for transfers between devices: 189 us -> 203 us  [local(): router_grad = lax.psum(lax.psum(router_term, 'ctx'), 'dp')]
  transfers between devices with their start and end apart: 8 -> 9, of which waited for: 7 -> 7; matrix products, arithmetic and copies ran while one was open for 11% -> 12% of each run, Pallas kernels for 0% -> 0%
where the time goes in v1:
time: 947 us; the launch traced here: 943 us
  waiting for transfers between devices  651 us (69%)
  blocking collectives  75.3 us (8%)
  local copies, waits for them, and re-layouts  60.3 us (6%)
  matrix products  58 us (6%)
  other arithmetic  47.4 us (5%)
  starting transfers between devices  36.6 us (4%)
  between operations  14.3 us (2%)
    psum x2, waiting for transfers between devices, local(): router_grad = lax.psum(lax.psum(router_term, 'ctx'), 'dp')  203 us
    all_to_all x2, waiting for transfers between devices, route_slots(): lax.all_to_all(outgoing, ('dp', 'ctx'), split_axis=0, concat_axis=0, tile...  113 us
    all_to_all x1, waiting for transfers between devices, local(): lax.all_to_all(expert_part, ('dp', 'ctx'), split_axis=0, concat_axis=0, t...  107 us
    psum x1, waiting for transfers between devices, local(): moe, dweight = lax.psum((moe_part, dweight_part), 'exp')  89 us
    psum x1, waiting for transfers between devices, local(): attention = lax.psum(head_part, 'exp')  83 us
    all_gather x1, blocking collectives, local(): lax.all_gather(doc_ids[0], 'ctx', axis=0, tiled=True)  37.8 us
    unnamed x2, other arithmetic  33.6 us
    all_to_all x1, waiting for transfers between devices, from_everyone(): lax.all_to_all(jnp.broadcast_to(array[None], (count, *array.shape)), axis...  29.8 us
  transfers between devices with their start and end apart: 9, of which 7 were waited for; matrix products, arithmetic and copies ran while one was open for 12% of the time, Pallas kernels for 0%

profile of v1, /device:TPU:88, one launch (start us, length us, event | category | flops | bytes accessed | tf_op | source)
XLA Modules:
  0.0 942.9 jit_solution(2001715051286146553)
XLA Ops:
  10.4 5.8 all-to-all-start
  16.3 29.8 %all-to-all-done = f32[8,128,576]{1,2,0:T(8,128)} async-done(((f32[8,128,576]{1,2,0:T(8,128)}), f32[8,128,576]{1,2,0:T(8,128)}, u32[]{:S(2)}, u32[]{:S(2)}) %all-to-all-start) | async-done | bytes 2359328 | tf_op jit(solution)/shard_map/all_to_all | solution.py:13
  49.0 37.8 %all-gather = s32[1,2048]{1,0:T(1,128)S(1)} all-gather(s32[1,128]{1,0:T(1,128)S(1)} %copy-done.4), channel_id=2, replica_groups=mesh['dp'=2,'ctx'=16,'exp'=8] {'ctx'}, dimensions={1}, use_global_device_ids=true | all-gather | bytes 8704 | tf_op jit(solution)/shard_map/all_gather | solution.py:93
  87.1 26.5 %all-gather.3.cloned.1.call-done = bf16[2048,576]{0,1:T(8,128)(2,1)} async-done(((bf16[128,576]{0,1:T(8,128)(2,1)}), bf16[2048,576]{0,1:T(8,128)(2,1)}) %all-gather.3.cloned.1.call-update) | async-done | bytes 2359312 | tf_op jit(solution)/shard_map/all_gather | solution.py:92
  126.0 83.0 %all-reduce.5.cloned.1.call-done = f32[128,2560]{1,0:T(8,128)} async-done(((f32[128,2560]{1,0:T(8,128)}), f32[128,2560]{1,0:T(8,128)}) %all-reduce.5.cloned.1.call-update) | async-done | bytes 1310736 | tf_op jit(solution)/shard_map/psum | solution.py:124
  214.7 8.9 all-to-all-start.1
  223.7 113.3 %all-to-all-done.1 = bf16[32,1,32,2560]{3,2,1,0:T(8,128)(2,1)} async-done(((bf16[32,1,32,2560]{3,2,1,0:T(8,128)(2,1)}), bf16[32,1,32,2560]{3,2,1,0:T(8,128)(2,1)}, u32[]{:S(2)}, u32[]{:S(2)}) %all-to-all-start.1) | async-done | bytes 5242912 | tf_op jit(solution)/shard_map/all_to_all | solution.py:56
  341.4 5.4 multiply_convert_fusion.2
  351.4 12.1 %all-to-all-start.2 = ((bf16[32,1,32,2560]{3,2,1,0:T(8,128)(2,1)}), bf16[32,1,32,2560]{3,2,1,0:T(8,128)(2,1)}, u32[]{:S(2)}, u32[]{:S(2)}) async-start(bf16[32,1,32,2560]{3,2,1,0:T(8,128)(2,1)} %fusion.13), calls=%async_computation.2 | async-start | bytes 10485760 | tf_op jit(solution)/shard_map/all_to_all | solution.py:177
  364.6 5.1 gather_fusion
  370.0 107.0 %all-to-all-done.2 = bf16[32,1,32,2560]{3,2,1,0:T(8,128)(2,1)} async-done(((bf16[32,1,32,2560]{3,2,1,0:T(8,128)(2,1)}), bf16[32,1,32,2560]{3,2,1,0:T(8,128)(2,1)}, u32[]{:S(2)}, u32[]{:S(2)}) %all-to-all-start.2) | async-done | bytes 5242912 | tf_op jit(solution)/shard_map/all_to_all | solution.py:177
  481.1 5.1 gather_fusion.1
  486.4 23.5 %psum.37 = f32[128,6]{0,1:T(8,128)S(1)} all-reduce(f32[128,6]{0,1:T(8,128)S(1)} %and_select_fusion), channel_id=1, replica_groups=mesh['dp'=2,'ctx'=16,'exp'=8] {'exp'}, use_global_device_ids=true, to_apply=%region_15.16 | all-reduce | flops 768 | bytes 6144 | tf_op jit(solution)/shard_map/psum | solution.py:183
  510.4 5.0 convolution_convert_fusion
  515.4 9.6 %all-to-all-start.3 = ((bf16[32,1,32,2560]{3,2,1,0:T(8,128)(2,1)}), bf16[32,1,32,2560]{3,2,1,0:T(8,128)(2,1)}, u32[]{:S(2)}, u32[]{:S(2)}) async-start(bf16[32,1,32,2560]{3,2,1,0:T(8,128)(2,1)} %bitcast.236), calls=%async_computation.3 | async-start | bytes 10485760 | tf_op jit(solution)/shard_map/all_to_all | solution.py:56
  530.9 202.5 %all-reduce.9.cloned.1.call-done = f32[2560,32]{0,1:T(8,128)} async-done(((f32[2560,32]{0,1:T(8,128)}), f32[2560,32]{0,1:T(8,128)}) %all-reduce.9.cloned.1.call-update) | async-done | bytes 327696 | tf_op jit(solution)/shard_map/psum | solution.py:193
  733.5 89.0 %all-reduce.7.cloned.1.call-done = f32[128,2560]{1,0:T(8,128)} async-done(((f32[128,2560]{1,0:T(8,128)}), f32[128,2560]{1,0:T(8,128)}) %all-reduce.7.cloned.1.call-update) | async-done | bytes 1310736 | tf_op jit(solution)/shard_map/psum | solution.py:183
  838.0 8.9 copy.117
  847.5 18.2 %reduce.3 = bf16[2560,384]{1,0:T(8,128)(2,1)} reduce(bf16[2560,1,384]{2,1,0:T(2,128)(2,1)} %bitcast.237, bf16[]{:T(256)} %broadcast.489), dimensions={1}, to_apply=%bitcast.212.reduce_sub_computation | reduce | bytes 3932162
  868.5 8.4 all_to_all.50
  893.5 6.3 copy.118
  899.9 15.4 %reduce.4 = bf16[2560,192]{1,0:T(8,128)(2,1)S(1)} reduce(bf16[2560,1,192]{2,1,0:T(2,128)(2,1)} %bitcast.241, bf16[]{:T(256)} %broadcast.489), dimensions={1}, to_apply=%bitcast.214.reduce_sub_computation | reduce | bytes 1966082
  917.6 5.6 all_to_all.51
  926.1 5.1 copy.119
  (115 shorter events, 91.3 us)
Async XLA Ops:
  7.2 340.4 %copy-start = (bf16[2,192,2560]{2,1,0:T(8,128)(2,1)S(1)}, bf16[2,192,2560]{2,1,0:T(8,128)(2,1)}, u32[]{:S(2)}) copy-start(bf16[2,192,2560]{2,1,0:T(8,128)(2,1)} %param.26) | copy-start | bytes 5898244
  10.4 5.9 copy-start.5
  10.4 35.7 %all-to-all-start = ((f32[8,128,576]{1,2,0:T(8,128)}), f32[8,128,576]{1,2,0:T(8,128)}, u32[]{:S(2)}, u32[]{:S(2)}) async-start(f32[8,128,576]{1,2,0:T(8,128)} %broadcast_in_dim.34), calls=%async_computation | async-start | bytes 4718592 | tf_op jit(solution)/shard_map/all_to_all | solution.py:13
  16.1 32.8 %copy-start.4 = (s32[1,128]{1,0:T(1,128)S(1)}, s32[1,128]{1,0:T(1,128)}, u32[]{:S(2)}) copy-start(s32[1,128]{1,0:T(1,128)} %param.23) | copy-start | bytes 1540
  16.2 97.5 %copy-start.7 = (bf16[1,128,2,576]{1,3,2,0:T(8,128)(2,1)S(1)}, bf16[1,128,2,576]{1,3,2,0:T(8,128)(2,1)}, u32[]{:S(2)}) copy-start(bf16[1,128,2,576]{1,3,2,0:T(8,128)(2,1)} %param.15) | copy-start | bytes 884740
  16.2 97.4 %all-gather.3.cloned.1.call-start = ((), (), s32[]{:S(2)}) async-start(), calls=%async_computation.6 | async-start | bytes 2506752 | tf_op jit(solution)/shard_map/all_gather | solution.py:92
  48.9 160.1 %all-reduce.5.cloned.1.call-start = ((), (), s32[]{:S(2)}) async-start(), calls=%async_computation.7 | async-start | bytes 2621440 | tf_op jit(solution)/shard_map/psum | solution.py:124
  118.3 2.9 copy-start.1
  121.2 1.5 copy-start.2
  121.2 4.3 copy-start.3
  214.7 122.2 %all-to-all-start.1 = ((bf16[32,1,32,2560]{3,2,1,0:T(8,128)(2,1)}), bf16[32,1,32,2560]{3,2,1,0:T(8,128)(2,1)}, u32[]{:S(2)}, u32[]{:S(2)}) async-start(bf16[32,1,32,2560]{3,2,1,0:T(8,128)(2,1)} %bitcast.235), calls=%async_computation.1 | async-start | bytes 10485760 | tf_op jit(solution)/shard_map/all_to_all | solution.py:56
  336.9 4.5 copy-start.6
  341.4 5.4 copy-start.9
  346.8 0.8 copy-start.12
  351.4 12.7 %copy-start.8 = (bf16[2560,32]{0,1:T(8,128)(2,1)S(1)}, bf16[2560,32]{0,1:T(8,128)(2,1)}, u32[]{:S(2)}) copy-start(bf16[2560,32]{0,1:T(8,128)(2,1)} %param.21) | copy-start | bytes 491524
  351.4 125.5 %all-to-all-start.2 = ((bf16[32,1,32,2560]{3,2,1,0:T(8,128)(2,1)}), bf16[32,1,32,2560]{3,2,1,0:T(8,128)(2,1)}, u32[]{:S(2)}, u32[]{:S(2)}) async-start(bf16[32,1,32,2560]{3,2,1,0:T(8,128)(2,1)} %fusion.13), calls=%async_computation.2 | async-start | bytes 10485760 | tf_op jit(solution)/shard_map/all_to_all | solution.py:177
  515.4 309.4 %all-to-all-start.3 = ((bf16[32,1,32,2560]{3,2,1,0:T(8,128)(2,1)}), bf16[32,1,32,2560]{3,2,1,0:T(8,128)(2,1)}, u32[]{:S(2)}, u32[]{:S(2)}) async-start(bf16[32,1,32,2560]{3,2,1,0:T(8,128)(2,1)} %bitcast.236), calls=%async_computation.3 | async-start | bytes 10485760 | tf_op jit(solution)/shard_map/all_to_all | solution.py:56
  525.0 208.5 %all-reduce.9.cloned.1.call-start = ((), (), s32[]{:S(2)}) async-start(), calls=%async_computation.9 | async-start | bytes 655360 | tf_op jit(solution)/shard_map/psum | solution.py:193
  526.4 296.1 %all-reduce.7.cloned.1.call-start = ((), (), s32[]{:S(2)}) async-start(), calls=%async_computation.8 | async-start | bytes 2621440 | tf_op jit(solution)/shard_map/psum | solution.py:183
  530.9 403.8 %all-reduce.11.cloned.1.call-start = ((), (), s32[]{:S(2)}) async-start(), calls=%async_computation.10 | async-start | bytes 655360 | tf_op jit(solution)/shard_map/psum | solution.py:193
  824.8 4.1 copy-start.10
  828.9 3.9 copy-start.11
  881.1 2.5 copy-start.13
Sparse Core Ops, SparseCore 0:
  49.1 64.4 all-gather.2
  122.8 86.1 all-reduce.4
  529.0 204.4 all-reduce.8
  736.0 86.4 all-reduce.6
  824.9 28.3 all-reduce.10
